TPU v7x, 32 devices: a whole 2x2x4 slice. The times are simulated.
32 devices in a mesh: groups: 2 (over x), ep: 16 (over z, y, core).
Axes of the slice: x: 2, y: 2, z: 4, core: 2. Of those that a mesh axis runs over, the one named last changes fastest.
Arguments:
- tokens: bfloat16 [1024, 3584], P(('groups', 'ep')), parts along dimension 0, may hold values from -6 to 6
- routes: int32 [1024, 8], P(('groups', 'ep')), parts along dimension 0, may hold values from 0 to 255, all different within a row; in each aligned block of 32 rows (0 to 31, 32 to 63, ...) at most 2 rows name the same one
- gate_num: int32 [1024, 8], P(('groups', 'ep')), parts along dimension 0, may hold values from 1 to 255
- w_gate: bfloat16 [16, 3584, 512], P('ep'), may hold values from -0.09375 to 0.09375
- w_up: bfloat16 [16, 3584, 512], P('ep'), may hold values from -0.09375 to 0.09375
- w_down: bfloat16 [16, 512, 3584], P('ep'), may hold values from -0.1875 to 0.1875
Outputs:
- combined: bfloat16 [1024, 3584], P(('groups', 'ep')), parts along dimension 0
There are 2 independent parts, one for each index of `groups`. A program takes and returns all parts, laid end to end along the dimension named above; an argument that names none is the same for every part. Nothing has to cross between parts.
Inputs may be any that keep to these rules, and one draw needn't show every extreme that they name: `routes`: each row names 8 different experts; among the 32 rows of one device no expert is named more than 2 times, a bound that some block reaches.
All inputs are finite; a program needn't handle non-finite values.
Results may differ from a plain program's by a relative error of at most 0.0058.
Values may be sent and summed in bfloat16 or wider, within the bound.
No kernel may reach another device: no remote copies, remote signals or barrier semaphores. Data moves between devices by JAX's collectives and lax.ppermute only.
A program may use at most 64 MiB of HBM per device.

v0:
```python
import jax
import jax.numpy as jnp
from jax import lax
from jax.sharding import PartitionSpec as P

SPLIT = 2
EXPERTS = 256


def partner_2(block, axis, apart):
    count = lax.axis_size(axis)
    route = []
    for low in range(count):
        high = low | 1 << apart
        if high != low and high < count:
            route += [(low, high), (high, low)]
    return lax.ppermute(block, axis, route)


def expert_mlp(received, w_gate, w_up, w_down):
    local_count = w_gate.shape[0]
    senders = received.shape[0] // local_count
    slot_count = received.shape[1]
    feature_width = received.shape[2]
    blocks = received.reshape(senders, local_count, slot_count, feature_width)
    gate_part = jnp.einsum("secd,edf->secf", blocks, w_gate, preferred_element_type=jnp.float32)
    up_part = jnp.einsum("secd,edf->secf", blocks, w_up, preferred_element_type=jnp.float32)
    hidden = (jax.nn.silu(gate_part) * up_part).astype(jnp.bfloat16)
    output = jnp.einsum("secf,efd->secd", hidden, w_down, preferred_element_type=jnp.float32)
    return output.reshape(senders * local_count, slot_count, feature_width)


def serve_rows(received, w_gate, w_up, w_down):
    parity = lax.axis_index("ep") % 2
    partner = partner_2(received, "ep", 0)
    lower_rows = jnp.where(parity == 0, received, partner)
    upper_rows = jnp.where(parity == 0, partner, received)
    whole_rows = jnp.concatenate([lower_rows, upper_rows], axis=2)
    results = expert_mlp(whole_rows, w_gate, w_up, w_down)
    half_width = results.shape[2] // 2
    lower_out = results[:, :, :half_width]
    upper_out = results[:, :, half_width:]
    kept = jnp.where(parity == 0, lower_out, upper_out)
    sending = jnp.where(parity == 0, upper_out, lower_out)
    arrived = partner_2(sending, "ep", 0)
    summed = (kept + arrived).astype(jnp.bfloat16)
    return lax.all_to_all(summed, "ep", split_axis=0, concat_axis=0, tiled=True)


def shards(tokens, routes, gate_num, w_gate, w_up, w_down):
    tok_rows, top_count = routes.shape
    feature_width = tokens.shape[1]
    devices_all = lax.axis_size("ep")
    experts_all = devices_all // SPLIT
    capacity = max(2, min(tok_rows, 5 * tok_rows * top_count // (2 * EXPERTS)))
    flat_routes = routes.reshape(-1)
    served = flat_routes < experts_all
    one_hot = (flat_routes[:, None] == jnp.arange(experts_all, dtype=jnp.int32)[None, :]).astype(
        jnp.int32
    )
    before = jnp.cumsum(one_hot, axis=0) - one_hot
    position = jnp.sum(before * one_hot, axis=1)
    slot_total = experts_all * capacity
    slot_index = jnp.where(served, flat_routes * capacity + position, slot_total)
    token_of = jnp.arange(tok_rows * top_count, dtype=jnp.int32) // top_count
    source_row = jnp.zeros((slot_total,), jnp.int32).at[slot_index].set(token_of, mode="drop")
    filled = jnp.zeros((slot_total,), jnp.bool_).at[slot_index].set(True, mode="drop")
    outgoing = jnp.where(filled[:, None], tokens[source_row], jnp.zeros((), tokens.dtype))
    outgoing = outgoing.reshape(experts_all, capacity, feature_width)
    half_width = feature_width // SPLIT
    outgoing = outgoing.reshape(experts_all, capacity, SPLIT, half_width)
    outgoing = outgoing.transpose(0, 2, 1, 3).reshape(experts_all * SPLIT, capacity, half_width)
    received = lax.all_to_all(outgoing, "ep", split_axis=0, concat_axis=0, tiled=True)
    returned = serve_rows(received, w_gate, w_up, w_down)
    returned = returned.reshape(experts_all, SPLIT, capacity, half_width)
    expert_rows = returned.transpose(0, 2, 1, 3).reshape(experts_all, capacity, feature_width)
    safe_route = jnp.where(served, flat_routes, 0)
    picked = expert_rows[safe_route, position]
    picked = picked.reshape(tok_rows, top_count, feature_width)
    gate_real = jnp.where(
        served.reshape(tok_rows, top_count), gate_num.astype(jnp.float32) / 256.0, 0.0
    )
    weights = gate_real.astype(jnp.bfloat16)
    combined = jnp.einsum("tk,tkd->td", weights, picked, preferred_element_type=jnp.float32)
    return combined.astype(jnp.bfloat16)


def solution(mesh):
    return jax.shard_map(
        shards,
        mesh=mesh,
        in_specs=(
            P(("groups", "ep"), None),
            P(("groups", "ep"), None),
            P(("groups", "ep"), None),
            P("ep", None, None),
            P("ep", None, None),
            P("ep", None, None),
        ),
        out_specs=P(("groups", "ep"), None),
        check_vma=False,
    )
```

profile of v0, /device:TPU:0, one launch (start us, length us, event | category | flops | bytes accessed | tf_op | source)
XLA Modules:
  0.0 48.8 jit_solution(16190040157651471799)
XLA Ops:
  0.0 0.0 copy-start
  0.0 0.8 %copy.16 = s32[32,8]{1,0:T(8,128)S(1)} copy(s32[32,8]{0,1:T(8,128)} %param.7) | data formatting | bytes 2048 | tf_op args[1]
  0.8 0.1 eq.38
  0.9 0.1 eq.34
  1.0 0.1 reshape.134
  1.1 0.6 %reduce-window.6 = s32[8,2,128]{2,0,1:T(8,128)S(1)} reduce-window(s32[8,2,128]{2,0,1:T(8,128)S(1)} %fusion.22, s32[]{:T(128)} %constant.50.clone.1), window={size=1x1x128 pad=0_0x0_0x127_0}, to_apply=%region_0.0 | reduce-window | flops 260096 | bytes 16388 | tf_op jit(solution)/shard_map/reduce-window
  1.7 0.2 slice_reduce_fusion
  1.9 0.1 fusion.21
  2.0 1.4 %scatter_custom_fusion.1 = s32[16]{0:T(128)S(1)} fusion(s32[256]{0:T(256)S(1)} %bitcast.73, s32[256]{0:T(256)S(1)} %and_select_fusion, s32[]{:T(128)} %constant.50.clone.1), kind=kCustom, calls=%fused_computation.52 | custom fusion | bytes 68 | tf_op jit(solution)/shard_map/scatter | solution.py:66
  3.5 1.5 %scatter_custom_fusion = pred[16]{0:T(512)(128)(4,1)S(1)} fusion(s32[256]{0:T(256)S(1)} %bitcast.74, pred[256]{0:T(512)(128)(4,1)S(1)} %broadcast.151, pred[]{:T(512)} %constant.53.clone.1), kind=kCustom, calls=%fused_computation.50 | custom fusion | bytes 17 | tf_op jit(solution)/shard_map/scatter | solution.py:67
  5.0 0.1 broadcast_in_dim.38
  5.1 0.0 copy-done
  5.1 0.6 %gather_fusion = bf16[16,3584]{1,0:T(8,128)(2,1)S(1)} fusion(bf16[32,3584]{1,0:T(8,128)(2,1)S(1)} %copy-done, s32[1024]{0:T(1024)S(1)} %pad_clamp_fusion), kind=kCustom, calls=%fused_computation | custom fusion | bytes 229440 | tf_op jit(solution)/shard_map/gather | solution.py:68
  5.7 0.2 fusion.14
  5.9 0.1 copy.19
  6.0 14.9 %all_to_all.10 = bf16[16,2,1792]{2,1,0:T(2,128)(2,1)S(1)} all-to-all(bf16[16,2,1792]{2,1,0:T(2,128)(2,1)S(1)} %bitcast.70), channel_id=1, replica_groups=mesh['groups'=2,'ep'=16] {'ep'}, dimensions={0} | all-to-all | bytes 229376 | tf_op jit(solution)/shard_map/all_to_all | solution.py:73
  20.9 0.1 collective-permute-start
  21.0 1.3 %collective-permute-done = bf16[16,2,1792]{2,0,1:T(8,128)(2,1)S(1)} collective-permute-done((bf16[16,2,1792]{2,0,1:T(8,128)(2,1)S(1)}, bf16[16,2,1792]{2,0,1:T(8,128)(2,1)S(1)}, u32[]{:S(2)}, u32[]{:S(2)}) %collective-permute-start) | collective-permute-done | bytes 114720 | tf_op jit(solution)/shard_map/ppermute | solution.py:17
  22.3 2.8 %fusion.8 = f32[16,1,2,512]{3,0,2,1:T(8,128)S(1)} fusion(bf16[1,3584,512]{2,1,0:T(8,128)(2,1)} %param.9, bf16[16,2,1792]{2,0,1:T(8,128)(2,1)S(1)} %get-tuple-element.6, bf16[16,2,1792]{2,0,1:T(8,128)(2,1)S(1)} %get-tuple-element.5), kind=kOutput, calls=%fused_computation.12 | convolution fusion | flops 117899264 | bytes 3964928 | tf_op jit(solution)/shard_map/secd,edf->secf/dot_general | solution.py:26
  25.1 0.0 copy-start.1
  25.1 0.0 copy-start.2
  25.1 4.6 %fusion = f32[16,2,3584]{2,0,1:T(8,128)S(1)} fusion(bf16[1,512,3584]{2,1,0:T(8,128)(2,1)} %param.11, f32[16,1,2,512]{3,0,2,1:T(8,128)S(1)} %fusion.8, bf16[1,3584,512]{2,1,0:T(8,128)(2,1)} %param.10, bf16[16,2,1792]{2,0,1:T(8,128)(2,1)S(1)} %get-tuple-element.6, bf16[16,2,1792]{2,0,1:T(8,128)(2,1)S(1)} %get-tuple-element.5), kind=kOutput, calls=%fused_computation.4 | convolution fusion | flops 235438080 | bytes 8093696 | tf_op jit(solution)/shard_map/secf,efd->secd/dot_general | solution.py:29
  29.7 0.2 collective-permute-start.1
  29.9 1.3 %collective-permute-done.1 = f32[16,2,1792]{2,0,1:T(8,128)S(1)} collective-permute-done((f32[16,2,1792]{2,0,1:T(8,128)S(1)}, f32[16,2,1792]{2,0,1:T(8,128)S(1)}, u32[]{:S(2)}, u32[]{:S(2)}) %collective-permute-start.1) | collective-permute-done | bytes 229408 | tf_op jit(solution)/shard_map/ppermute | solution.py:17
  31.3 0.7 %copy.23 = bf16[16,2,1792]{2,1,0:T(2,128)(2,1)} copy(bf16[16,2,1792]{2,0,1:T(8,128)(2,1)S(1)} %add_convert_fusion) | data formatting | bytes 229376 | tf_op jit(solution)/shard_map/convert_element_type | solution.py:46
  32.0 3.5 %all-to-all-start.1 = ((bf16[16,2,1792]{2,1,0:T(2,128)(2,1)}), bf16[16,2,1792]{2,1,0:T(2,128)(2,1)S(1)}, u32[]{:S(2)}, u32[]{:S(2)}) async-start(bf16[16,2,1792]{2,1,0:T(2,128)(2,1)} %copy.23), calls=%async_computation.1 | async-start | bytes 229376 | tf_op jit(solution)/shard_map/all_to_all | solution.py:47
  35.6 0.0 copy-done.1
  35.6 0.0 copy-done.2
  35.6 0.1 copy.25
  35.7 7.5 %all-to-all-done.1 = bf16[16,2,1792]{2,1,0:T(2,128)(2,1)S(1)} async-done(((bf16[16,2,1792]{2,1,0:T(2,128)(2,1)}), bf16[16,2,1792]{2,1,0:T(2,128)(2,1)S(1)}, u32[]{:S(2)}, u32[]{:S(2)}) %all-to-all-start.1) | async-done | bytes 114720 | tf_op jit(solution)/shard_map/all_to_all | solution.py:47
  43.2 0.1 copy.32
  43.3 0.1 reshape.142
  43.3 4.1 %gather_fusion.1 = bf16[256,3584]{1,0:T(8,128)(2,1)S(1)} fusion(bf16[8,2,3584]{2,1,0:T(2,128)(2,1)S(1)} %reshape.142, s32[256]{0:T(256)S(1)} %bitcast.68), kind=kCustom, calls=%fused_computation.1 | custom fusion | bytes 3672064 | tf_op jit(solution)/shard_map/gather | solution.py:78
  47.5 0.6 %fusion.6 = bf16[32,1,3584]{2,1,0:T(2,128)(2,1)S(1)} fusion(bf16[32,8,1]{1,2,0:T(2,128)(2,1)S(1)} %copy.25, bf16[256,3584]{1,0:T(8,128)(2,1)S(1)} %gather_fusion.1), kind=kOutput, calls=%fused_computation.10 | convolution fusion | flops 1835008 | bytes 2064896 | tf_op jit(solution)/shard_map/tk,tkd->td/dot_general | solution.py:84
  48.1 0.7 %copy.31 = bf16[32,1,3584]{2,0,1:T(8,128)(2,1)} copy(bf16[32,1,3584]{2,1,0:T(2,128)(2,1)S(1)} %fusion.6) | data formatting | bytes 458752 | tf_op jit(solution)/shard_map/tk,tkd->td/dot_general | solution.py:84
  (14 shorter events, 0.2 us)
Async XLA Ops:
  0.0 5.1 %copy-start = (bf16[32,3584]{1,0:T(8,128)(2,1)S(1)}, bf16[32,3584]{1,0:T(8,128)(2,1)}, u32[]{:S(2)}) copy-start(bf16[32,3584]{1,0:T(8,128)(2,1)} %param.6) | copy-start | bytes 688132
  20.9 1.4 %collective-permute-start = (bf16[16,2,1792]{2,0,1:T(8,128)(2,1)S(1)}, bf16[16,2,1792]{2,0,1:T(8,128)(2,1)S(1)}, u32[]{:S(2)}, u32[]{:S(2)}) collective-permute-start(bf16[16,2,1792]{2,0,1:T(8,128)(2,1)S(1)} %copy.21), channel_id=1, source_target_pairs={{0,1},{1,0},{2,3},{3,2},{4,5},{5,4},{6,7},{7,6},{8,9},{9,8},{10,11... | collective-permute-start | bytes 344072 | tf_op jit(solution)/shard_map/ppermute | solution.py:17
  25.1 10.5 %copy-start.1 = (s32[32,8]{0,1:T(8,128)S(1)}, s32[32,8]{0,1:T(8,128)}, u32[]{:S(2)}) copy-start(s32[32,8]{0,1:T(8,128)} %param.7) | copy-start | bytes 3076
  25.1 10.5 %copy-start.2 = (s32[32,8]{0,1:T(8,128)S(1)}, s32[32,8]{0,1:T(8,128)}, u32[]{:S(2)}) copy-start(s32[32,8]{0,1:T(8,128)} %param.8) | copy-start | bytes 3076
  29.7 1.6 %collective-permute-start.1 = (f32[16,2,1792]{2,0,1:T(8,128)S(1)}, f32[16,2,1792]{2,0,1:T(8,128)S(1)}, u32[]{:S(2)}, u32[]{:S(2)}) collective-permute-start(f32[16,2,1792]{2,0,1:T(8,128)S(1)} %slice_select_fusion), channel_id=1, source_target_pairs={{0,1},{1,0},{2,3},{3,2},{4,5},{5,4},{6,7},{7,6},{8,9},{9,8},{10,11... | collective-permute-start | bytes 688136 | tf_op jit(solution)/shard_map/ppermute | solution.py:17
  32.0 11.1 %all-to-all-start.1 = ((bf16[16,2,1792]{2,1,0:T(2,128)(2,1)}), bf16[16,2,1792]{2,1,0:T(2,128)(2,1)S(1)}, u32[]{:S(2)}, u32[]{:S(2)}) async-start(bf16[16,2,1792]{2,1,0:T(2,128)(2,1)} %copy.23), calls=%async_computation.1 | async-start | bytes 229376 | tf_op jit(solution)/shard_map/all_to_all | solution.py:47
where the time goes:
time: 49.1 us; the launch traced here: 48.8 us
  blocking collectives  14.9 us (30%)
  local copies, waits for them, and re-layouts  10.9 us (22%)
  waiting for transfers between devices  10.1 us (21%)
  matrix products  7.98 us (16%)
  starting transfers between devices  3.8 us (8%)
  other arithmetic  1.01 us (2%)
    all_to_all x1, blocking collectives, shards(): lax.all_to_all(outgoing, 'ep', split_axis=0, concat_axis=0, tiled=True)  14.9 us
    all_to_all x1, waiting for transfers between devices, serve_rows(): return lax.all_to_all(summed, 'ep', split_axis=0, concat_axis=0, tiled=True)  7.48 us
    dot_general x1, matrix products, expert_mlp(): jnp.einsum('secf,efd->secd', hidden, w_down, preferred_element_type=jnp.f...  4.61 us
    gather x1, local copies, waits for them, and re-layouts, shards(): picked = expert_rows[safe_route, position]  4.12 us
    all_to_all x1, starting transfers between devices, serve_rows(): return lax.all_to_all(summed, 'ep', split_axis=0, concat_axis=0, tiled=True)  3.51 us
    dot_general x1, matrix products, expert_mlp(): jnp.einsum('secd,edf->secf', blocks, w_gate, preferred_element_type=jnp.f...  2.76 us
    ppermute x2, waiting for transfers between devices, partner_2(): return lax.ppermute(block, axis, route)  2.64 us
    scatter x1, local copies, waits for them, and re-layouts, shards(): jnp.zeros((slot_total,), jnp.bool_).at[slot_index].set(True, mode='drop')  1.49 us
  transfers between devices with their start and end apart: 3, of which 3 were waited for; matrix products, arithmetic and copies ran while one was open for 0% of the time, Pallas kernels for 0%

commit v1 on v0

--- a/solution.py
+++ b/solution.py
@@ -70,7 +70,19 @@
     half_width = feature_width // SPLIT
     outgoing = outgoing.reshape(experts_all, capacity, SPLIT, half_width)
     outgoing = outgoing.transpose(0, 2, 1, 3).reshape(experts_all * SPLIT, capacity, half_width)
-    received = lax.all_to_all(outgoing, "ep", split_axis=0, concat_axis=0, tiled=True)
+    ways, here = (lax.axis_size("ep"), lax.axis_index("ep"))
+    width = outgoing.shape[0] // ways
+    shape = list(outgoing.shape)
+    shape[0] = width
+    height = shape[0]
+    shape[0] = height * ways
+    full = jnp.zeros(shape, outgoing.dtype)
+    for mask in range(ways):
+        part = lax.dynamic_slice_in_dim(outgoing, (here ^ mask) * width, width, axis=0)
+        if mask:
+            part = lax.ppermute(part, "ep", [(d, d ^ mask) for d in range(ways)])
+        full = lax.dynamic_update_slice_in_dim(full, part, (here ^ mask) * height, axis=0)
+    received = full
     returned = serve_rows(received, w_gate, w_up, w_down)
     returned = returned.reshape(experts_all, SPLIT, capacity, half_width)
     expert_rows = returned.transpose(0, 2, 1, 3).reshape(experts_all, capacity, feature_width)

time: 49.1 us -> 62.2 us (1.27)
  starting transfers between devices: 3.8 us -> 25.8 us
  blocking collectives: 14.9 us -> 0 us
  waiting for transfers between devices: 10.1 us -> 13.4 us
  local copies, waits for them, and re-layouts: 10.9 us -> 13.3 us
    ppermute x0 -> x15, starting transfers between devices: none -> 21.9 us  [shards(): part = lax.ppermute(part, 'ep', [(d, d ^ mask) for d in range(ways)])]
    all_to_all x1 -> x0, blocking collectives: 14.9 us -> none  [shards(): lax.all_to_all(outgoing, 'ep', split_axis=0, concat_axis=0, tiled=True)]
    ppermute x0 -> x15, waiting for transfers between devices: none -> 3.4 us  [shards(): part = lax.ppermute(part, 'ep', [(d, d ^ mask) for d in range(ways)])]
    dynamic_update_slice x0 -> x16, local copies, waits for them, and re-layouts: none -> 2.01 us  [shards(): lax.dynamic_update_slice_in_dim(full, part, (here ^ mask) * height, axis=0)]
  transfers between devices with their start and end apart: 3 -> 18, of which waited for: 3 -> 5; matrix products, arithmetic and copies ran while one was open for 0% -> 3% of each run, Pallas kernels for 0% -> 0%
where the time goes in v1:
time: 62.2 us; the launch traced here: 62 us
  starting transfers between devices  25.8 us (41%)
  waiting for transfers between devices  13.4 us (22%)
  local copies, waits for them, and re-layouts  13.3 us (21%)
  matrix products  7.98 us (13%)
  other arithmetic  1.03 us (2%)
    ppermute x15, starting transfers between devices, shards(): part = lax.ppermute(part, 'ep', [(d, d ^ mask) for d in range(ways)])  21.9 us
    all_to_all x1, waiting for transfers between devices, serve_rows(): return lax.all_to_all(summed, 'ep', split_axis=0, concat_axis=0, tiled=True)  7.48 us
    dot_general x1, matrix products, expert_mlp(): jnp.einsum('secf,efd->secd', hidden, w_down, preferred_element_type=jnp.f...  4.61 us
    gather x1, local copies, waits for them, and re-layouts, shards(): picked = expert_rows[safe_route, position]  4.12 us
    all_to_all x1, starting transfers between devices, serve_rows(): return lax.all_to_all(summed, 'ep', split_axis=0, concat_axis=0, tiled=True)  3.51 us
    ppermute x15, waiting for transfers between devices, shards(): part = lax.ppermute(part, 'ep', [(d, d ^ mask) for d in range(ways)])  3.4 us
    dot_general x1, matrix products, expert_mlp(): jnp.einsum('secd,edf->secf', blocks, w_gate, preferred_element_type=jnp.f...  2.76 us
    ppermute x2, waiting for transfers between devices, partner_2(): return lax.ppermute(block, axis, route)  2.55 us
  transfers between devices with their start and end apart: 18, of which 5 were waited for; matrix products, arithmetic and copies ran while one was open for 3% of the time, Pallas kernels for 0%

profile of v1, /device:TPU:0, one launch (start us, length us, event | category | flops | bytes accessed | tf_op | source)
XLA Modules:
  0.0 62.0 jit_solution(7883498515940150093)
XLA Ops:
  0.0 0.8 %copy.16 = s32[32,8]{1,0:T(8,128)S(1)} copy(s32[32,8]{0,1:T(8,128)} %param.7) | data formatting | bytes 2048 | tf_op args[1]
  0.8 0.1 eq.38
  0.9 0.1 eq.34
  1.0 0.1 reshape.134
  1.1 0.6 reduce-window.6
  1.7 0.2 slice_reduce_fusion
  1.9 0.1 fusion.21
  2.0 1.4 %scatter_custom_fusion.1 = s32[16]{0:T(128)S(1)} fusion(s32[256]{0:T(256)S(1)} %bitcast.73, s32[256]{0:T(256)S(1)} %and_select_fusion, s32[]{:T(128)} %constant.30.clone.1), kind=kCustom, calls=%fused_computation.68 | custom fusion | bytes 68 | tf_op jit(solution)/shard_map/scatter | solution.py:66
  3.5 1.5 %scatter_custom_fusion = pred[16]{0:T(512)(128)(4,1)S(1)} fusion(s32[256]{0:T(256)S(1)} %bitcast.74, pred[256]{0:T(512)(128)(4,1)S(1)} %broadcast.154, pred[]{:T(512)} %constant.34.clone.1), kind=kCustom, calls=%fused_computation.66 | custom fusion | bytes 17 | tf_op jit(solution)/shard_map/scatter | solution.py:67
  5.0 0.1 broadcast_in_dim.42
  5.1 0.1 copy.19
  5.2 0.6 gather_fusion
  5.8 0.2 fusion.14
  6.1 0.4 constant_dynamic-slice_fusion
  6.5 5.1 %collective-permute-start.9 = (bf16[1,2,1792]{2,0,1:T(2,128)(2,1)S(1)}, bf16[1,2,1792]{2,0,1:T(2,128)(2,1)S(1)}, u32[]{:S(2)}, u32[]{:S(2)}) collective-permute-start(bf16[1,2,1792]{2,0,1:T(2,128)(2,1)S(1)} %get-tuple-element.12), channel_id=1, source_target_pairs={{0,10},{1,11},{2,8},{3,9},{4,14},{5,15},{6,12},{7,13},{8,2},{9,3},... | collective-permute-start | bytes 21512 | tf_op jit(solution)/shard_map/ppermute | solution.py:83
  11.6 2.1 %collective-permute-start.7 = (bf16[1,2,1792]{2,0,1:T(2,128)(2,1)S(1)}, bf16[1,2,1792]{2,0,1:T(2,128)(2,1)S(1)}, u32[]{:S(2)}, u32[]{:S(2)}) collective-permute-start(bf16[1,2,1792]{2,0,1:T(2,128)(2,1)S(1)} %get-tuple-element.14), channel_id=1, source_target_pairs={{0,8},{1,9},{2,10},{3,11},{4,12},{5,13},{6,14},{7,15},{8,0},{9,1},... | collective-permute-start | bytes 21512 | tf_op jit(solution)/shard_map/ppermute | solution.py:83
  13.7 1.8 %collective-permute-start.6 = (bf16[1,2,1792]{2,0,1:T(2,128)(2,1)S(1)}, bf16[1,2,1792]{2,0,1:T(2,128)(2,1)S(1)}, u32[]{:S(2)}, u32[]{:S(2)}) collective-permute-start(bf16[1,2,1792]{2,0,1:T(2,128)(2,1)S(1)} %get-tuple-element.15), channel_id=1, source_target_pairs={{0,7},{1,6},{2,5},{3,4},{4,3},{5,2},{6,1},{7,0},{8,15},{9,14},{10,... | collective-permute-start | bytes 21512 | tf_op jit(solution)/shard_map/ppermute | solution.py:83
  15.5 1.4 %collective-permute-start.5 = (bf16[1,2,1792]{2,0,1:T(2,128)(2,1)S(1)}, bf16[1,2,1792]{2,0,1:T(2,128)(2,1)S(1)}, u32[]{:S(2)}, u32[]{:S(2)}) collective-permute-start(bf16[1,2,1792]{2,0,1:T(2,128)(2,1)S(1)} %get-tuple-element.16), channel_id=1, source_target_pairs={{0,6},{1,7},{2,4},{3,5},{4,2},{5,3},{6,0},{7,1},{8,14},{9,15},{10,... | collective-permute-start | bytes 21512 | tf_op jit(solution)/shard_map/ppermute | solution.py:83
  16.9 0.7 %collective-permute-start.4 = (bf16[1,2,1792]{2,0,1:T(2,128)(2,1)S(1)}, bf16[1,2,1792]{2,0,1:T(2,128)(2,1)S(1)}, u32[]{:S(2)}, u32[]{:S(2)}) collective-permute-start(bf16[1,2,1792]{2,0,1:T(2,128)(2,1)S(1)} %get-tuple-element.17), channel_id=1, source_target_pairs={{0,5},{1,4},{2,7},{3,6},{4,1},{5,0},{6,3},{7,2},{8,13},{9,12},{10,... | collective-permute-start | bytes 21512 | tf_op jit(solution)/shard_map/ppermute | solution.py:83
  17.7 0.9 %collective-permute-start.3 = (bf16[1,2,1792]{2,0,1:T(2,128)(2,1)S(1)}, bf16[1,2,1792]{2,0,1:T(2,128)(2,1)S(1)}, u32[]{:S(2)}, u32[]{:S(2)}) collective-permute-start(bf16[1,2,1792]{2,0,1:T(2,128)(2,1)S(1)} %get-tuple-element.18), channel_id=1, source_target_pairs={{0,4},{1,5},{2,6},{3,7},{4,0},{5,1},{6,2},{7,3},{8,12},{9,13},{10,... | collective-permute-start | bytes 21512 | tf_op jit(solution)/shard_map/ppermute | solution.py:83
  18.6 0.0 collective-permute-done.7
  18.6 0.3 collective-permute-start.2
  18.9 1.5 %collective-permute-start.1 = (bf16[1,2,1792]{2,0,1:T(2,128)(2,1)S(1)}, bf16[1,2,1792]{2,0,1:T(2,128)(2,1)S(1)}, u32[]{:S(2)}, u32[]{:S(2)}) collective-permute-start(bf16[1,2,1792]{2,0,1:T(2,128)(2,1)S(1)} %get-tuple-element.20), channel_id=1, source_target_pairs={{0,2},{1,3},{2,0},{3,1},{4,6},{5,7},{6,4},{7,5},{8,10},{9,11},{10,... | collective-permute-start | bytes 21512 | tf_op jit(solution)/shard_map/ppermute | solution.py:83
  20.4 0.0 collective-permute-start
  20.4 1.4 %collective-permute-start.12 = (bf16[1,2,1792]{2,0,1:T(2,128)(2,1)S(1)}, bf16[1,2,1792]{2,0,1:T(2,128)(2,1)S(1)}, u32[]{:S(2)}, u32[]{:S(2)}) collective-permute-start(bf16[1,2,1792]{2,0,1:T(2,128)(2,1)S(1)} %get-tuple-element.9), channel_id=1, source_target_pairs={{0,13},{1,12},{2,15},{3,14},{4,9},{5,8},{6,11},{7,10},{8,5},{9,4},... | collective-permute-start | bytes 21512 | tf_op jit(solution)/shard_map/ppermute | solution.py:83
  21.9 1.3 %collective-permute-start.10 = (bf16[1,2,1792]{2,0,1:T(2,128)(2,1)S(1)}, bf16[1,2,1792]{2,0,1:T(2,128)(2,1)S(1)}, u32[]{:S(2)}, u32[]{:S(2)}) collective-permute-start(bf16[1,2,1792]{2,0,1:T(2,128)(2,1)S(1)} %get-tuple-element.11), channel_id=1, source_target_pairs={{0,11},{1,10},{2,9},{3,8},{4,15},{5,14},{6,13},{7,12},{8,3},{9,2},... | collective-permute-start | bytes 21512 | tf_op jit(solution)/shard_map/ppermute | solution.py:83
  23.2 1.3 %collective-permute-start.11 = (bf16[1,2,1792]{2,0,1:T(2,128)(2,1)S(1)}, bf16[1,2,1792]{2,0,1:T(2,128)(2,1)S(1)}, u32[]{:S(2)}, u32[]{:S(2)}) collective-permute-start(bf16[1,2,1792]{2,0,1:T(2,128)(2,1)S(1)} %get-tuple-element.10), channel_id=1, source_target_pairs={{0,12},{1,13},{2,14},{3,15},{4,8},{5,9},{6,10},{7,11},{8,4},{9,5},... | collective-permute-start | bytes 21512 | tf_op jit(solution)/shard_map/ppermute | solution.py:83
  24.5 3.5 %collective-permute-start.13 = (bf16[1,2,1792]{2,0,1:T(2,128)(2,1)S(1)}, bf16[1,2,1792]{2,0,1:T(2,128)(2,1)S(1)}, u32[]{:S(2)}, u32[]{:S(2)}) collective-permute-start(bf16[1,2,1792]{2,0,1:T(2,128)(2,1)S(1)} %get-tuple-element.8), channel_id=1, source_target_pairs={{0,14},{1,15},{2,12},{3,13},{4,10},{5,11},{6,8},{7,9},{8,6},{9,7},... | collective-permute-start | bytes 21512 | tf_op jit(solution)/shard_map/ppermute | solution.py:83
  28.0 0.5 collective-permute-start.14
  28.5 0.1 dynamic_update_slice.48
  28.6 0.1 dynamic_update_slice.49
  28.8 0.1 dynamic_update_slice.50
  28.9 0.1 dynamic_update_slice.51
  29.0 0.1 dynamic_update_slice.52
  29.2 0.1 dynamic_update_slice.53
  29.3 0.1 dynamic_update_slice.54
  29.5 0.1 dynamic_update_slice.55
  29.6 0.1 dynamic_update_slice.56
  29.7 0.1 dynamic_update_slice.57
  29.9 0.1 dynamic_update_slice.58
  30.0 0.1 dynamic_update_slice.59
  30.2 0.1 dynamic_update_slice.60
  30.3 0.1 dynamic_update_slice.61
  30.5 0.5 collective-permute-done.13
  30.9 0.1 dynamic_update_slice.62
  31.0 2.9 %collective-permute-done.14 = bf16[1,2,1792]{2,0,1:T(2,128)(2,1)S(1)} collective-permute-done((bf16[1,2,1792]{2,0,1:T(2,128)(2,1)S(1)}, bf16[1,2,1792]{2,0,1:T(2,128)(2,1)S(1)}, u32[]{:S(2)}, u32[]{:S(2)}) %collective-permute-start.14) | collective-permute-done | bytes 7200 | tf_op jit(solution)/shard_map/ppermute | solution.py:83
  33.9 0.1 dynamic_update_slice.63
  34.0 0.2 collective-permute-start.15
  34.2 1.2 %collective-permute-done.15 = bf16[16,2,1792]{2,0,1:T(8,128)(2,1)S(1)} collective-permute-done((bf16[16,2,1792]{2,0,1:T(8,128)(2,1)S(1)}, bf16[16,2,1792]{2,0,1:T(8,128)(2,1)S(1)}, u32[]{:S(2)}, u32[]{:S(2)}) %collective-permute-start.15) | collective-permute-done | bytes 114720 | tf_op jit(solution)/shard_map/ppermute | solution.py:17
  35.4 2.8 %fusion.8 = f32[16,1,2,512]{3,0,2,1:T(8,128)S(1)} fusion(bf16[1,3584,512]{2,1,0:T(8,128)(2,1)} %param.9, bf16[16,2,1792]{2,0,1:T(8,128)(2,1)S(1)} %get-tuple-element.6, bf16[16,2,1792]{2,0,1:T(8,128)(2,1)S(1)} %get-tuple-element.5), kind=kOutput, calls=%fused_computation.12 | convolution fusion | flops 117899264 | bytes 3964928 | tf_op jit(solution)/shard_map/secd,edf->secf/dot_general | solution.py:26
  38.2 0.0 copy-start.2
  38.2 4.6 %fusion = f32[16,2,3584]{2,0,1:T(8,128)S(1)} fusion(bf16[1,512,3584]{2,1,0:T(8,128)(2,1)} %param.11, f32[16,1,2,512]{3,0,2,1:T(8,128)S(1)} %fusion.8, bf16[1,3584,512]{2,1,0:T(8,128)(2,1)} %param.10, bf16[16,2,1792]{2,0,1:T(8,128)(2,1)S(1)} %get-tuple-element.6, bf16[16,2,1792]{2,0,1:T(8,128)(2,1)S(1)} %get-tuple-element.5), kind=kOutput, calls=%fused_computation.4 | convolution fusion | flops 235438080 | bytes 8093696 | tf_op jit(solution)/shard_map/secf,efd->secd/dot_general | solution.py:29
  42.9 0.2 collective-permute-start.16
  43.1 1.3 %collective-permute-done.16 = f32[16,2,1792]{2,0,1:T(8,128)S(1)} collective-permute-done((f32[16,2,1792]{2,0,1:T(8,128)S(1)}, f32[16,2,1792]{2,0,1:T(8,128)S(1)}, u32[]{:S(2)}, u32[]{:S(2)}) %collective-permute-start.16) | collective-permute-done | bytes 229408 | tf_op jit(solution)/shard_map/ppermute | solution.py:17
  44.4 0.1 add_convert_fusion
  44.5 0.7 %copy.21 = bf16[16,2,1792]{2,1,0:T(2,128)(2,1)} copy(bf16[16,2,1792]{2,0,1:T(8,128)(2,1)S(1)} %add_convert_fusion) | data formatting | bytes 229376 | tf_op jit(solution)/shard_map/convert_element_type | solution.py:46
  45.2 3.5 %all-to-all-start = ((bf16[16,2,1792]{2,1,0:T(2,128)(2,1)}), bf16[16,2,1792]{2,1,0:T(2,128)(2,1)S(1)}, u32[]{:S(2)}, u32[]{:S(2)}) async-start(bf16[16,2,1792]{2,1,0:T(2,128)(2,1)} %copy.21), calls=%async_computation | async-start | bytes 229376 | tf_op jit(solution)/shard_map/all_to_all | solution.py:47
  48.8 0.1 copy.23
  48.9 7.5 %all-to-all-done = bf16[16,2,1792]{2,1,0:T(2,128)(2,1)S(1)} async-done(((bf16[16,2,1792]{2,1,0:T(2,128)(2,1)}), bf16[16,2,1792]{2,1,0:T(2,128)(2,1)S(1)}, u32[]{:S(2)}, u32[]{:S(2)}) %all-to-all-start) | async-done | bytes 114720 | tf_op jit(solution)/shard_map/all_to_all | solution.py:47
  56.3 0.1 copy.29
  56.4 0.1 reshape.142
  56.5 4.1 %gather_fusion.1 = bf16[256,3584]{1,0:T(8,128)(2,1)S(1)} fusion(bf16[8,2,3584]{2,1,0:T(2,128)(2,1)S(1)} %reshape.142, s32[256]{0:T(256)S(1)} %bitcast.69), kind=kCustom, calls=%fused_computation.1 | custom fusion | bytes 3672064 | tf_op jit(solution)/shard_map/gather | solution.py:90
  60.6 0.6 %fusion.6 = bf16[32,1,3584]{2,1,0:T(2,128)(2,1)S(1)} fusion(bf16[32,8,1]{1,2,0:T(2,128)(2,1)S(1)} %copy.23, bf16[256,3584]{1,0:T(8,128)(2,1)S(1)} %gather_fusion.1), kind=kOutput, calls=%fused_computation.10 | convolution fusion | flops 1835008 | bytes 2064896 | tf_op jit(solution)/shard_map/tk,tkd->td/dot_general | solution.py:96
  61.3 0.7 %copy.28 = bf16[32,1,3584]{2,0,1:T(8,128)(2,1)} copy(bf16[32,1,3584]{2,1,0:T(2,128)(2,1)S(1)} %fusion.6) | data formatting | bytes 458752 | tf_op jit(solution)/shard_map/tk,tkd->td/dot_general | solution.py:96
  (32 shorter events, 0.3 us)
Async XLA Ops:
  0.0 5.2 %copy-start = (bf16[32,3584]{1,0:T(8,128)(2,1)S(1)}, bf16[32,3584]{1,0:T(8,128)(2,1)}, u32[]{:S(2)}) copy-start(bf16[32,3584]{1,0:T(8,128)(2,1)} %param.6) | copy-start | bytes 688132
  6.5 10.4 %collective-permute-start.9 = (bf16[1,2,1792]{2,0,1:T(2,128)(2,1)S(1)}, bf16[1,2,1792]{2,0,1:T(2,128)(2,1)S(1)}, u32[]{:S(2)}, u32[]{:S(2)}) collective-permute-start(bf16[1,2,1792]{2,0,1:T(2,128)(2,1)S(1)} %get-tuple-element.12), channel_id=1, source_target_pairs={{0,10},{1,11},{2,8},{3,9},{4,14},{5,15},{6,12},{7,13},{8,2},{9,3},... | collective-permute-start | bytes 21512 | tf_op jit(solution)/shard_map/ppermute | solution.py:83
  11.6 6.0 %collective-permute-start.8 = (bf16[1,2,1792]{2,0,1:T(2,128)(2,1)S(1)}, bf16[1,2,1792]{2,0,1:T(2,128)(2,1)S(1)}, u32[]{:S(2)}, u32[]{:S(2)}) collective-permute-start(bf16[1,2,1792]{2,0,1:T(2,128)(2,1)S(1)} %get-tuple-element.13), channel_id=1, source_target_pairs={{0,9},{1,8},{2,11},{3,10},{4,13},{5,12},{6,15},{7,14},{8,1},{9,0},... | collective-permute-start | bytes 21512 | tf_op jit(solution)/shard_map/ppermute | solution.py:83
  11.6 6.9 %collective-permute-start.7 = (bf16[1,2,1792]{2,0,1:T(2,128)(2,1)S(1)}, bf16[1,2,1792]{2,0,1:T(2,128)(2,1)S(1)}, u32[]{:S(2)}, u32[]{:S(2)}) collective-permute-start(bf16[1,2,1792]{2,0,1:T(2,128)(2,1)S(1)} %get-tuple-element.14), channel_id=1, source_target_pairs={{0,8},{1,9},{2,10},{3,11},{4,12},{5,13},{6,14},{7,15},{8,0},{9,1},... | collective-permute-start | bytes 21512 | tf_op jit(solution)/shard_map/ppermute | solution.py:83
  13.7 5.2 %collective-permute-start.6 = (bf16[1,2,1792]{2,0,1:T(2,128)(2,1)S(1)}, bf16[1,2,1792]{2,0,1:T(2,128)(2,1)S(1)}, u32[]{:S(2)}, u32[]{:S(2)}) collective-permute-start(bf16[1,2,1792]{2,0,1:T(2,128)(2,1)S(1)} %get-tuple-element.15), channel_id=1, source_target_pairs={{0,7},{1,6},{2,5},{3,4},{4,3},{5,2},{6,1},{7,0},{8,15},{9,14},{10,... | collective-permute-start | bytes 21512 | tf_op jit(solution)/shard_map/ppermute | solution.py:83
  15.5 4.9 %collective-permute-start.5 = (bf16[1,2,1792]{2,0,1:T(2,128)(2,1)S(1)}, bf16[1,2,1792]{2,0,1:T(2,128)(2,1)S(1)}, u32[]{:S(2)}, u32[]{:S(2)}) collective-permute-start(bf16[1,2,1792]{2,0,1:T(2,128)(2,1)S(1)} %get-tuple-element.16), channel_id=1, source_target_pairs={{0,6},{1,7},{2,4},{3,5},{4,2},{5,3},{6,0},{7,1},{8,14},{9,15},{10,... | collective-permute-start | bytes 21512 | tf_op jit(solution)/shard_map/ppermute | solution.py:83
  16.9 3.5 %collective-permute-start.4 = (bf16[1,2,1792]{2,0,1:T(2,128)(2,1)S(1)}, bf16[1,2,1792]{2,0,1:T(2,128)(2,1)S(1)}, u32[]{:S(2)}, u32[]{:S(2)}) collective-permute-start(bf16[1,2,1792]{2,0,1:T(2,128)(2,1)S(1)} %get-tuple-element.17), channel_id=1, source_target_pairs={{0,5},{1,4},{2,7},{3,6},{4,1},{5,0},{6,3},{7,2},{8,13},{9,12},{10,... | collective-permute-start | bytes 21512 | tf_op jit(solution)/shard_map/ppermute | solution.py:83
  17.7 4.2 %collective-permute-start.3 = (bf16[1,2,1792]{2,0,1:T(2,128)(2,1)S(1)}, bf16[1,2,1792]{2,0,1:T(2,128)(2,1)S(1)}, u32[]{:S(2)}, u32[]{:S(2)}) collective-permute-start(bf16[1,2,1792]{2,0,1:T(2,128)(2,1)S(1)} %get-tuple-element.18), channel_id=1, source_target_pairs={{0,4},{1,5},{2,6},{3,7},{4,0},{5,1},{6,2},{7,3},{8,12},{9,13},{10,... | collective-permute-start | bytes 21512 | tf_op jit(solution)/shard_map/ppermute | solution.py:83
  18.6 4.6 %collective-permute-start.2 = (bf16[1,2,1792]{2,0,1:T(2,128)(2,1)S(1)}, bf16[1,2,1792]{2,0,1:T(2,128)(2,1)S(1)}, u32[]{:S(2)}, u32[]{:S(2)}) collective-permute-start(bf16[1,2,1792]{2,0,1:T(2,128)(2,1)S(1)} %get-tuple-element.19), channel_id=1, source_target_pairs={{0,3},{1,2},{2,1},{3,0},{4,7},{5,6},{6,5},{7,4},{8,11},{9,10},{10,... | collective-permute-start | bytes 21512 | tf_op jit(solution)/shard_map/ppermute | solution.py:83
  18.9 5.6 %collective-permute-start.1 = (bf16[1,2,1792]{2,0,1:T(2,128)(2,1)S(1)}, bf16[1,2,1792]{2,0,1:T(2,128)(2,1)S(1)}, u32[]{:S(2)}, u32[]{:S(2)}) collective-permute-start(bf16[1,2,1792]{2,0,1:T(2,128)(2,1)S(1)} %get-tuple-element.20), channel_id=1, source_target_pairs={{0,2},{1,3},{2,0},{3,1},{4,6},{5,7},{6,4},{7,5},{8,10},{9,11},{10,... | collective-permute-start | bytes 21512 | tf_op jit(solution)/shard_map/ppermute | solution.py:83
  20.4 7.6 %collective-permute-start = (bf16[1,2,1792]{2,0,1:T(2,128)(2,1)S(1)}, bf16[1,2,1792]{2,0,1:T(2,128)(2,1)S(1)}, u32[]{:S(2)}, u32[]{:S(2)}) collective-permute-start(bf16[1,2,1792]{2,0,1:T(2,128)(2,1)S(1)} %get-tuple-element.21), channel_id=1, source_target_pairs={{0,1},{1,0},{2,3},{3,2},{4,5},{5,4},{6,7},{7,6},{8,9},{9,8},{10,11... | collective-permute-start | bytes 21512 | tf_op jit(solution)/shard_map/ppermute | solution.py:83
  20.4 9.9 %collective-permute-start.12 = (bf16[1,2,1792]{2,0,1:T(2,128)(2,1)S(1)}, bf16[1,2,1792]{2,0,1:T(2,128)(2,1)S(1)}, u32[]{:S(2)}, u32[]{:S(2)}) collective-permute-start(bf16[1,2,1792]{2,0,1:T(2,128)(2,1)S(1)} %get-tuple-element.9), channel_id=1, source_target_pairs={{0,13},{1,12},{2,15},{3,14},{4,9},{5,8},{6,11},{7,10},{8,5},{9,4},... | collective-permute-start | bytes 21512 | tf_op jit(solution)/shard_map/ppermute | solution.py:83
  21.9 8.1 %collective-permute-start.10 = (bf16[1,2,1792]{2,0,1:T(2,128)(2,1)S(1)}, bf16[1,2,1792]{2,0,1:T(2,128)(2,1)S(1)}, u32[]{:S(2)}, u32[]{:S(2)}) collective-permute-start(bf16[1,2,1792]{2,0,1:T(2,128)(2,1)S(1)} %get-tuple-element.11), channel_id=1, source_target_pairs={{0,11},{1,10},{2,9},{3,8},{4,15},{5,14},{6,13},{7,12},{8,3},{9,2},... | collective-permute-start | bytes 21512 | tf_op jit(solution)/shard_map/ppermute | solution.py:83
  23.2 7.0 %collective-permute-start.11 = (bf16[1,2,1792]{2,0,1:T(2,128)(2,1)S(1)}, bf16[1,2,1792]{2,0,1:T(2,128)(2,1)S(1)}, u32[]{:S(2)}, u32[]{:S(2)}) collective-permute-start(bf16[1,2,1792]{2,0,1:T(2,128)(2,1)S(1)} %get-tuple-element.10), channel_id=1, source_target_pairs={{0,12},{1,13},{2,14},{3,15},{4,8},{5,9},{6,10},{7,11},{8,4},{9,5},... | collective-permute-start | bytes 21512 | tf_op jit(solution)/shard_map/ppermute | solution.py:83
  24.5 6.4 %collective-permute-start.13 = (bf16[1,2,1792]{2,0,1:T(2,128)(2,1)S(1)}, bf16[1,2,1792]{2,0,1:T(2,128)(2,1)S(1)}, u32[]{:S(2)}, u32[]{:S(2)}) collective-permute-start(bf16[1,2,1792]{2,0,1:T(2,128)(2,1)S(1)} %get-tuple-element.8), channel_id=1, source_target_pairs={{0,14},{1,15},{2,12},{3,13},{4,10},{5,11},{6,8},{7,9},{8,6},{9,7},... | collective-permute-start | bytes 21512 | tf_op jit(solution)/shard_map/ppermute | solution.py:83
  28.0 5.9 %collective-permute-start.14 = (bf16[1,2,1792]{2,0,1:T(2,128)(2,1)S(1)}, bf16[1,2,1792]{2,0,1:T(2,128)(2,1)S(1)}, u32[]{:S(2)}, u32[]{:S(2)}) collective-permute-start(bf16[1,2,1792]{2,0,1:T(2,128)(2,1)S(1)} %get-tuple-element.7), channel_id=1, source_target_pairs={{0,15},{1,14},{2,13},{3,12},{4,11},{5,10},{6,9},{7,8},{8,7},{9,6},... | collective-permute-start | bytes 21512 | tf_op jit(solution)/shard_map/ppermute | solution.py:83
  34.0 1.4 %collective-permute-start.15 = (bf16[16,2,1792]{2,0,1:T(8,128)(2,1)S(1)}, bf16[16,2,1792]{2,0,1:T(8,128)(2,1)S(1)}, u32[]{:S(2)}, u32[]{:S(2)}) collective-permute-start(bf16[16,2,1792]{2,0,1:T(8,128)(2,1)S(1)} %dynamic_update_slice.63), channel_id=1, source_target_pairs={{0,1},{1,0},{2,3},{3,2},{4,5},{5,4},{6,7},{7,6},{8,9},{9,8},{10,11... | collective-permute-start | bytes 344072 | tf_op jit(solution)/shard_map/ppermute | solution.py:17
  38.2 10.5 %copy-start.1 = (s32[32,8]{0,1:T(8,128)S(1)}, s32[32,8]{0,1:T(8,128)}, u32[]{:S(2)}) copy-start(s32[32,8]{0,1:T(8,128)} %param.7) | copy-start | bytes 3076
  38.2 10.5 %copy-start.2 = (s32[32,8]{0,1:T(8,128)S(1)}, s32[32,8]{0,1:T(8,128)}, u32[]{:S(2)}) copy-start(s32[32,8]{0,1:T(8,128)} %param.8) | copy-start | bytes 3076
  42.9 1.6 %collective-permute-start.16 = (f32[16,2,1792]{2,0,1:T(8,128)S(1)}, f32[16,2,1792]{2,0,1:T(8,128)S(1)}, u32[]{:S(2)}, u32[]{:S(2)}) collective-permute-start(f32[16,2,1792]{2,0,1:T(8,128)S(1)} %slice_select_fusion), channel_id=1, source_target_pairs={{0,1},{1,0},{2,3},{3,2},{4,5},{5,4},{6,7},{7,6},{8,9},{9,8},{10,11... | collective-permute-start | bytes 688136 | tf_op jit(solution)/shard_map/ppermute | solution.py:17
  45.2 11.1 %all-to-all-start = ((bf16[16,2,1792]{2,1,0:T(2,128)(2,1)}), bf16[16,2,1792]{2,1,0:T(2,128)(2,1)S(1)}, u32[]{:S(2)}, u32[]{:S(2)}) async-start(bf16[16,2,1792]{2,1,0:T(2,128)(2,1)} %copy.21), calls=%async_computation | async-start | bytes 229376 | tf_op jit(solution)/shard_map/all_to_all | solution.py:47
